TPU v7x, 256 devices: a whole 4x4x8 slice. The times are simulated.
256 devices in a mesh: tok: 64 (over y, z, x_hi), out: 4 (over x_lo, core).
Axes of the slice: x: 4 (x_hi: 2, x_lo: 2; x = x_hi * 2 + x_lo), y: 4, z: 8, core: 2. Of those that a mesh axis runs over, the one named last changes fastest.
Arguments:
- acts: bfloat16 [3, 4096, 8192], P(None, 'tok'), may hold values from -6 to 6
- grads: bfloat16 [3, 4096, 4096], P(None, 'tok', 'out'), may hold values from -6 to 6
- act_basis: float32 [1024, 8, 8], P('tok'), may hold values from -2 to 2
- grad_basis: float32 [512, 8, 8], P('out'), may hold values from -2 to 2
Outputs:
- eigen_corr: float32 [4096, 8192], P('out', 'tok')
All inputs are finite; a program needn't handle non-finite values.
Results may differ from a plain program's by a relative error of at most 0.014.
Values may be sent and summed in bfloat16 or wider, within the bound.
A program may use at most 128 MiB of HBM per device.

v0:
```python
import jax
import jax.numpy as jnp
from jax import lax
from jax.sharding import PartitionSpec as P


def rotate_local(values, basis):
    seqs, rows, width = values.shape
    span = min(128, width)
    count = span // 8
    groups = width // span
    blocks = basis.reshape(groups, count, 8, 8)
    identity = jnp.eye(count, dtype=jnp.float32)
    diagonal = (blocks[:, :, :, None, :] * identity[None, :, None, :, None]).reshape(
        groups, span, span
    )
    high_part = diagonal.astype(jnp.bfloat16)
    low_part = (diagonal - high_part.astype(jnp.float32)).astype(jnp.bfloat16)
    spread = values.reshape(seqs * rows, groups, span)
    turned = jnp.einsum("rgp,gpq->rgq", spread, high_part, preferred_element_type=jnp.float32)
    turned = turned + jnp.einsum(
        "rgp,gpq->rgq", spread, low_part, preferred_element_type=jnp.float32
    )
    return turned.reshape(seqs, rows, width).astype(jnp.bfloat16)


def shards(acts, grads, act_basis, grad_basis):
    turned_acts = rotate_local(
        lax.all_to_all(acts, "tok", split_axis=2, concat_axis=1, tiled=True), act_basis
    )
    turned_grads = rotate_local(grads, grad_basis)
    seqs, length, columns = turned_acts.shape
    scale = length ** (-0.5)
    products = jnp.einsum(
        "sto,sti->soi",
        lax.all_gather(turned_grads, "tok", axis=1, tiled=True),
        turned_acts,
        preferred_element_type=jnp.float32,
    )
    scaled = products * scale
    return jnp.sum(scaled * scaled, axis=0)


def solution(mesh):
    placed = (
        P(None, "tok", None),
        P(None, "tok", "out"),
        P("tok", None, None),
        P("out", None, None),
    )
    return jax.shard_map(
        shards, mesh=mesh, in_specs=placed, out_specs=P("out", "tok"), check_vma=False
    )
```

profile of v0, /device:TPU:1, one launch (start us, length us, event | category | flops | bytes accessed | tf_op | source)
XLA Modules:
  0.0 358.7 jit_solution(10031555253662685400)
XLA Ops:
  6.5 1.1 copy.35
  7.6 1.0 copy.32
  8.6 0.1 mul.72
  8.8 0.5 mul.73
  9.2 3.9 %mul.70 = f32[8,16,8,16,8]{4,3,2,1,0:T(8,128)} broadcast(f32[8,16,8,8]{3,2,1,0:T(8,128)S(1)} %bitcast.39), dimensions={0,1,2,4} | broadcast | bytes 557056 | tf_op jit(solution)/shard_map/mul | solution.py:14
  13.2 6.4 %mul.71 = f32[8,128,128]{2,1,0:T(8,128)S(1)} reshape(f32[8,16,8,16,8]{4,3,2,1,0:T(8,128)} %mul.70) | data formatting | bytes 1048576 | tf_op jit(solution)/shard_map/mul | solution.py:14
  19.5 0.3 fusion.5
  19.8 0.3 fusion.3
  20.1 0.3 copy.26
  20.3 0.9 convert_element_type.96
  21.3 11.2 %copy.28 = bf16[3,64,8192]{1,0,2:T(4,128)(2,1)} copy(bf16[3,64,8192]{2,1,0:T(8,128)(2,1)} %param.4) | data formatting | bytes 6291456 | tf_op args[0]
  32.5 13.4 %reshape.77 = bf16[64,2,12288]{2,1,0:T(2,128)(2,1)} reshape(bf16[8192,3,64]{2,1,0:T(4,128)(2,1)} %bitcast.33) | data formatting | bytes 6291456
  45.9 15.4 %all-to-all-start = ((bf16[64,2,12288]{2,1,0:T(2,128)(2,1)}), bf16[64,2,12288]{2,1,0:T(2,128)(2,1)S(1)}, u32[]{:S(2)}, u32[]{:S(2)}) async-start(bf16[64,2,12288]{2,1,0:T(2,128)(2,1)} %reshape.77), calls=%async_computation | async-start | bytes 6291456 | tf_op jit(solution)/shard_map/all_to_all | solution.py:29
  61.4 1.2 fusion.4
  62.6 1.5 convert_element_type.101
  64.1 1.5 convert_element_type.98
  65.6 94.4 %all-to-all-done = bf16[64,2,12288]{2,1,0:T(2,128)(2,1)S(1)} async-done(((bf16[64,2,12288]{2,1,0:T(2,128)(2,1)}), bf16[64,2,12288]{2,1,0:T(2,128)(2,1)S(1)}, u32[]{:S(2)}, u32[]{:S(2)}) %all-to-all-start) | async-done | bytes 3145760 | tf_op jit(solution)/shard_map/all_to_all | solution.py:29
  160.0 9.2 %reshape.78 = bf16[8192,3,64]{2,1,0:T(4,128)(2,1)} reshape(bf16[64,2,12288]{2,1,0:T(2,128)(2,1)S(1)} %all-to-all-done) | data formatting | bytes 6291456
  169.2 10.5 %copy.34 = bf16[3,64,64,128]{3,1,2,0:T(8,128)(2,1)S(1)} copy(bf16[3,64,64,128]{1,0,3,2:T(4,128)(2,1)} %bitcast.32) | data formatting | bytes 6291456 | tf_op jit(solution)/shard_map/all_to_all | solution.py:29
  179.7 1.0 fusion.11
  180.7 3.2 fusion.1
  183.9 3.9 %copy.31 = bf16[12288,1,128]{2,0,1:T(8,128)(2,1)S(1)} copy(bf16[12288,1,128]{0,2,1:T(8,128)(2,1)} %fusion.1) | data formatting | bytes 6291456 | tf_op jit(solution)/shard_map/convert_element_type | solution.py:24
  187.8 149.6 %all-gather.2.cloned.1.call-done = bf16[3,4096,1024]{2,1,0:T(8,128)(2,1)} async-done(((bf16[3,64,1024]{2,1,0:T(8,128)(2,1)}), bf16[3,4096,1024]{2,1,0:T(8,128)(2,1)}) %all-gather.2.cloned.1.call-update) | async-done | bytes 25165840 | tf_op jit(solution)/shard_map/all_gather | solution.py:36
  337.3 14.5 %multiply_reduce_fusion = f32[1024,128]{1,0:T(8,128)} fusion(bf16[3,4096,1024]{2,1,0:T(8,128)(2,1)} %all-gather.2.cloned.1.call-done, bf16[3,4096,128]{2,1,0:T(8,128)(2,1)S(1)} %bitcast.36), kind=kOutput, calls=%fused_computation.3 | convolution fusion | flops 3222274048 | bytes 28835840 | tf_op jit(solution)/shard_map/sto,sti->soi/dot_general | solution.py:34
  (6 shorter events, 0.1 us)
Async XLA Ops:
  6.5 330.8 %all-gather.2.cloned.1.call-start = ((), (), s32[]{:S(2)}) async-start(), calls=%async_computation.1 | async-start | bytes 25559040 | tf_op jit(solution)/shard_map/all_gather | solution.py:36
  45.9 15.4 %copy-start = (f32[16,8,8]{0,2,1:T(8,128)S(1)}, f32[16,8,8]{0,2,1:T(8,128)}, u32[]{:S(2)}) copy-start(f32[16,8,8]{0,2,1:T(8,128)} %param.6) | copy-start | bytes 12292
  45.9 114.1 %all-to-all-start = ((bf16[64,2,12288]{2,1,0:T(2,128)(2,1)}), bf16[64,2,12288]{2,1,0:T(2,128)(2,1)S(1)}, u32[]{:S(2)}, u32[]{:S(2)}) async-start(bf16[64,2,12288]{2,1,0:T(2,128)(2,1)} %reshape.77), calls=%async_computation | async-start | bytes 6291456 | tf_op jit(solution)/shard_map/all_to_all | solution.py:29
Sparse Core Ops, SparseCore 0:
  21.4 315.8 all-gather.1
where the time goes:
time: 360 us; the launch traced here: 359 us
  waiting for transfers between devices  244 us (68%)
  local copies, waits for them, and re-layouts  65.4 us (18%)
  matrix products  19.2 us (5%)
  starting transfers between devices  15.4 us (4%)
  between operations  13.5 us (4%)
    all_gather x1, waiting for transfers between devices, shards(): lax.all_gather(turned_grads, 'tok', axis=1, tiled=True)  150 us
    all_to_all x1, waiting for transfers between devices, shards(): lax.all_to_all(acts, 'tok', split_axis=2, concat_axis=1, tiled=True)  94.4 us
    unnamed x7, local copies, waits for them, and re-layouts  35 us
    all_to_all x1, starting transfers between devices, shards(): lax.all_to_all(acts, 'tok', split_axis=2, concat_axis=1, tiled=True)  15.4 us
    dot_general x1, matrix products, shards(): jnp.einsum('sto,sti->soi', lax.all_gather(turned_grads, 'tok', axis=1, ti...  14.5 us
    mul x5, local copies, waits for them, and re-layouts, rotate_local(): blocks[:, :, :, None, :] * identity[None, :, None, :, None]  11.9 us
    all_to_all x1, local copies, waits for them, and re-layouts, shards(): lax.all_to_all(acts, 'tok', split_axis=2, concat_axis=1, tiled=True)  10.5 us
  transfers between devices with their start and end apart: 2, of which 2 were waited for; matrix products, arithmetic and copies ran while one was open for 16% of the time, Pallas kernels for 0%

commit v1 on v0

v1 whole, which is shorter than its diff:
```python
import functools

import jax
import jax.numpy as jnp
from jax import lax
from jax.experimental import pallas as pl
from jax.experimental.pallas import tpu as pltpu
from jax.sharding import PartitionSpec as P

MESH = pl.DeviceIdType.MESH
Y, Z, X = 4, 8, 4
BF16, F32 = jnp.bfloat16, jnp.float32


def gather_kernel(
    acts, grads, out,
    a2, a_all, a_t, g_all, snd, rcv, own, fin, landed,
    a_send, a_recv, w_send, l_send, s_send, g_recv, k_send, k_recv,
    x_send, x_recv, y_send, y_recv, f_send, f_recv, o_sem,
):
    seqs, rows, _ = acts.shape
    width = a2.shape[-1]
    half = width // 2
    tok, place = lax.axis_index("tok"), lax.axis_index("out")
    xh, z, y = lax.rem(tok, 2), lax.rem(lax.div(tok, 2), Z), lax.div(tok, 2 * Z)
    c, xl = lax.rem(place, 2), lax.div(place, 2)
    x = 2 * xh + xl
    sgn = 1 - 2 * c
    chunk = 2 * xl + c

    def dev(xi, yi, zi, ci):
        return ((yi * Z + zi) * 2 + lax.div(xi, 2), 2 * lax.rem(xi, 2) + ci)

    swapped = ((y * Z + z) * 2 + c, 2 * xl + xh)
    stays = xh == c

    def remote(src, dst, send, recv, device):
        return pltpu.make_async_remote_copy(
            src_ref=src, dst_ref=dst, send_sem=send, recv_sem=recv,
            device_id=device, device_id_type=MESH,
        )

    def arrived(ref, sem):
        pltpu.make_async_copy(ref, ref, sem).wait()

    barrier = pltpu.get_barrier_semaphore()

    def greet(device):
        pl.semaphore_signal(barrier, inc=1, device_id=device, device_id_type=MESH)

    @pl.loop(1, Z)
    def _(d):
        greet(dev(x, y, lax.rem(z + d, Z), c))

    @pl.loop(1, Y)
    def _(d):
        greet(dev(x, lax.rem(y + d, Y), z, c))

    @pl.loop(1, 2 * X)
    def _(d):
        greet(dev(lax.rem(x + lax.div(d, 2), X), y, z, lax.rem(c + d, 2)))

    pl.semaphore_wait(barrier, (Z - 1) + (Y - 1) + (2 * X - 1))

    def a2a(s):
        def view(zi):
            col = pl.multiple_of((chunk * Z + zi) * width, width)
            return acts.at[s, :, pl.ds(col, width)]

        @pl.loop(1, Z)
        def _(d):
            zt = lax.rem(z + d, Z)
            remote(view(zt), a2.at[s, z], a_send.at[s, d], a_recv.at[s, z],
                   dev(x, y, zt, c)).start()

        pltpu.make_async_copy(view(z), a2.at[s, z], a_recv.at[s, z]).start()

    def to_swapped(s, wait=False):
        copy = remote(grads.at[s], g_all.at[s, xh, z], w_send.at[s], g_recv.at[s, z], swapped)
        if wait:
            @pl.when(jnp.logical_not(stays))
            def _():
                copy.wait_send()
            return

        @pl.when(stays)
        def _():
            pltpu.make_async_copy(grads.at[s], g_all.at[s, c, z], g_recv.at[s, z]).start()

        @pl.when(jnp.logical_not(stays))
        def _():
            copy.start()

    def block(k):
        return lax.rem(z + k * sgn + Z, Z)

    def ring(s, zz, direction, sem):
        return remote(g_all.at[s, c, zz], g_all.at[s, c, zz], sem, g_recv.at[s, zz],
                      dev(x, y, lax.rem(z + direction + Z, Z), c))

    def long(s, k):
        return ring(s, block(-k), sgn, l_send.at[s, k])

    def short(s, k):
        return ring(s, block(k), -sgn, s_send.at[s, k])

    def across(s, zz):
        return remote(g_all.at[s, c, zz], g_all.at[s, c, zz], k_send.at[s, zz], k_recv.at[s, zz],
                      dev(x, y, z, 1 - c))

    def ring_start(s):
        arrived(g_all.at[s, c, z], g_recv.at[s, z])
        long(s, 0).start()
        short(s, 0).start()
        across(s, z).start()

    def ring_rest(s):
        for k in range(1, 5):
            zz = block(-k)
            arrived(g_all.at[s, c, zz], g_recv.at[s, zz])
            if k < 4:
                long(s, k).start()
            across(s, zz).start()
            if k < 4:
                zz = block(k)
                arrived(g_all.at[s, c, zz], g_recv.at[s, zz])
                if k < 3:
                    short(s, k).start()
                across(s, zz).start()

    def x_copy(s, d):
        h = lax.rem(c + d, 2)
        cols = pl.ds(pl.multiple_of(h * half, half), half)
        return remote(a2.at[s, :, :, cols], a_all.at[s, chunk, xh], x_send.at[s, d],
                      x_recv.at[s, chunk, xh], dev(lax.rem(x + lax.div(d, 2), X), y, z, h))

    def xsend(s):
        @pl.loop(0, Z)
        def _(zz):
            arrived(a2.at[s, zz], a_recv.at[s, zz])

        @pl.loop(1, 2 * X)
        def _(d):
            x_copy(s, d).start()

        cols = pl.ds(pl.multiple_of(c * half, half), half)
        pltpu.make_async_copy(a2.at[s, :, :, cols], a_all.at[s, chunk, xh],
                              x_recv.at[s, chunk, xh]).start()

    def y_copy(s, d):
        yt = lax.rem(y + d, Y)
        return remote(snd.at[s, yt], rcv.at[s, y], y_send.at[s, d], y_recv.at[s, y],
                      dev(x, yt, z, c))

    def compute(s):
        depth = 2 * Z * rows
        for yi in range(Y):
            for t in range(2):
                arrived(a_all.at[s, yi, t], x_recv.at[s, yi, t])
            a_t[yi * half:(yi + 1) * half, :] = a_all[s, yi].reshape(depth, half).T

        @pl.loop(0, Z)
        def _(zz):
            arrived(g_all.at[s, 1 - c, zz], k_recv.at[s, zz])

        @pl.loop(0, 4)
        def _(n):
            cols = pl.ds(pl.multiple_of(n * 256, 256), 256)
            g = g_all[s, :, :, :, cols].reshape(depth, 256)
            r = jnp.dot(a_t[...], g, preferred_element_type=F32)
            for yi in range(Y):
                piece = r[yi * half:(yi + 1) * half]
                snd[s, yi, :, cols] = piece.astype(BF16)

                @pl.when(y == yi)
                def _():
                    own[s, :, cols] = piece

        for d in (2, 1, 3):
            y_copy(s, d).start()

    def f_copy(s):
        return remote(fin.at[s], landed.at[s], f_send.at[s], f_recv.at[s], swapped)

    def reduce(s):
        for d in (1, 3, 2):
            yt = lax.rem(y + d, Y)
            arrived(rcv.at[s, yt], y_recv.at[s, yt])

        @pl.loop(0, half // 16)
        def _(i):
            part = pl.ds(pl.multiple_of(i * 16, 16), 16)
            total = own[s, part, :]
            for d in range(1, Y):
                total = total + rcv[s, lax.rem(y + d, Y), part, :].astype(F32)
            fin[s, part, :] = total.astype(BF16)

        @pl.when(stays)
        def _():
            pltpu.make_async_copy(fin.at[s], landed.at[s], f_recv.at[s]).start()

        @pl.when(jnp.logical_not(stays))
        def _():
            f_copy(s).start()

    for s in range(seqs):
        to_swapped(s)
    a2a(0)
    ring_start(0)
    a2a(1)
    xsend(0)
    ring_rest(0)
    ring_start(1)
    a2a(2)
    xsend(1)
    compute(0)
    ring_rest(1)
    ring_start(2)
    xsend(2)
    compute(1)
    ring_rest(2)
    reduce(0)
    compute(2)
    reduce(1)
    reduce(2)
    for s in range(seqs):
        arrived(landed.at[s], f_recv.at[s])
        pltpu.make_async_copy(landed.at[s], out.at[s], o_sem.at[s]).start()

    @pl.loop(0, seqs)
    def _(s):
        to_swapped(s, wait=True)

        @pl.loop(1, Z)
        def _(d):
            col = pl.multiple_of(chunk * width, width)
            remote(acts.at[s, :, pl.ds(col, width)], a2.at[s, z], a_send.at[s, d],
                   a_recv.at[s, z], swapped).wait_send()

        for k in range(4):
            long(s, k).wait_send()
            if k < 3:
                short(s, k).wait_send()

        @pl.loop(0, Z)
        def _(zz):
            across(s, zz).wait_send()

        @pl.loop(1, 2 * X)
        def _(d):
            x_copy(s, d).wait_send()

        @pl.loop(1, Y)
        def _(d):
            y_copy(s, d).wait_send()

        @pl.when(jnp.logical_not(stays))
        def _():
            f_copy(s).wait_send()

        pltpu.make_async_copy(landed.at[s], out.at[s], o_sem.at[s]).wait()


def gathered(acts, grads):
    seqs, rows, _ = acts.shape
    units = grads.shape[2]
    width = acts.shape[2] // (Y * Z)
    half = width // 2
    dma = pltpu.SemaphoreType.DMA
    return pl.pallas_call(
        gather_kernel,
        out_shape=jax.ShapeDtypeStruct((seqs, half, units), BF16),
        in_specs=[pl.BlockSpec(memory_space=pl.ANY)] * 2,
        out_specs=pl.BlockSpec(memory_space=pl.ANY),
        scratch_shapes=[
            pltpu.VMEM((seqs, Z, rows, width), BF16),
            pltpu.VMEM((seqs, Y, 2, Z, rows, half), BF16),
            pltpu.VMEM((Y * half, 2 * Z * rows), BF16),
            pltpu.VMEM((seqs, 2, Z, rows, units), BF16),
            pltpu.VMEM((seqs, Y, half, units), BF16),
            pltpu.VMEM((seqs, Y, half, units), BF16),
            pltpu.VMEM((seqs, half, units), F32),
            pltpu.VMEM((seqs, half, units), BF16),
            pltpu.VMEM((seqs, half, units), BF16),
            dma((seqs, Z)), dma((seqs, Z)), dma((seqs,)),
            dma((seqs, 4)), dma((seqs, 3)), dma((seqs, Z)),
            dma((seqs, Z)), dma((seqs, Z)),
            dma((seqs, 2 * X)), dma((seqs, Y, 2)),
            dma((seqs, Y)), dma((seqs, Y)),
            dma((seqs,)), dma((seqs,)), dma((seqs,)),
        ],
        compiler_params=pltpu.CompilerParams(
            collective_id=0, has_side_effects=True, vmem_limit_bytes=56 << 20
        ),
        name="gathered",
    )(acts, grads)


def halves(v):
    high = v.astype(BF16)
    return high, (v - high.astype(F32)).astype(BF16)


def dot(a, b):
    return jnp.dot(a, b, preferred_element_type=F32)


def spread(basis):
    lane = lax.broadcasted_iota(jnp.int32, (8, 128), 1)
    pick = (lax.rem(lane, 8) == lax.broadcasted_iota(jnp.int32, (8, 128), 0)).astype(BF16)
    row = lax.div(lax.broadcasted_iota(jnp.int32, (128, 128), 0), 8)
    col = lax.div(lax.broadcasted_iota(jnp.int32, (128, 128), 1), 8)
    return [jnp.where(row == col, dot(part, pick), 0.0).astype(BF16) for part in halves(basis)]


def turn_kernel(corr, act_basis, grad_basis, out, *, scale):
    seqs, half, units = corr.shape
    act_high, act_low = spread(act_basis[...])
    act_high, act_low = act_high.T, act_low.T
    for j in range(units // 128):
        cols = slice(j * 128, (j + 1) * 128)
        grad_high, grad_low = spread(grad_basis[cols, :])
        total = jnp.zeros((half, 128), F32)
        for s in range(seqs):
            piece = corr[s, :, cols]
            high, low = halves(dot(piece, grad_high) + dot(piece, grad_low))
            turned = dot(act_high, high) + (dot(act_high, low) + dot(act_low, high))
            turned = turned * scale
            total = total + turned * turned
        out[cols, :] = total.T


def shards(acts, grads, act_basis, grad_basis):
    corr = gathered(acts, grads)
    length = acts.shape[1] * Y * Z * 2
    units = grads.shape[2]
    half = corr.shape[1]
    return pl.pallas_call(
        functools.partial(turn_kernel, scale=length ** -0.5),
        out_shape=jax.ShapeDtypeStruct((units, half), F32),
        name="turned",
    )(corr, act_basis.reshape(half, 8), grad_basis.reshape(units, 8))


def solution(mesh):
    placed = (
        P(None, "tok", None),
        P(None, "tok", "out"),
        P("tok", None, None),
        P("out", None, None),
    )
    return jax.shard_map(
        shards, mesh=mesh, in_specs=placed, out_specs=P("out", "tok"), check_vma=False
    )
```

time: 360 us -> 110 us (0.31)
  waiting for transfers between devices: 244 us -> 0 us
  Pallas kernels: 0 us -> 107 us
  local copies, waits for them, and re-layouts: 65.4 us -> 3.21 us
  matrix products: 19.2 us -> 0 us
  starting transfers between devices: 15.4 us -> 0 us
  between operations: 13.5 us -> 0.01 us
    all_gather x1 -> x0, waiting for transfers between devices: 150 us -> none  [shards(): lax.all_gather(turned_grads, 'tok', axis=1, tiled=True)]
    pallas_call x0 -> x2, Pallas kernels: none -> 107 us  [the longest x1 101 us: gathered(): pl.pallas_call(gather_kernel, out_shape=jax.ShapeDtypeStruct((seqs, half,...]
    all_to_all x1 -> x0, waiting for transfers between devices: 94.4 us -> none  [shards(): lax.all_to_all(acts, 'tok', split_axis=2, concat_axis=1, tiled=True)]
    unnamed x7 -> x2, local copies, waits for them, and re-layouts: 35 us -> 3.21 us
    dot_general x5 -> x0, matrix products: 19.2 us -> none  [the longest x1 14.5 us: shards(): jnp.einsum('sto,sti->soi', lax.all_gather(turned_grads, 'tok', axis=1, ti...]
    all_to_all x1 -> x0, starting transfers between devices: 15.4 us -> none  [shards(): lax.all_to_all(acts, 'tok', split_axis=2, concat_axis=1, tiled=True)]
    mul x5 -> x0, local copies, waits for them, and re-layouts: 11.9 us -> none  [rotate_local(): blocks[:, :, :, None, :] * identity[None, :, None, :, None]]
    all_to_all x1 -> x0, local copies, waits for them, and re-layouts: 10.5 us -> none  [shards(): lax.all_to_all(acts, 'tok', split_axis=2, concat_axis=1, tiled=True)]
  transfers between devices with their start and end apart: 2 -> 0, of which waited for: 2 -> 0; matrix products, arithmetic and copies ran while one was open for 16% -> 0% of each run, Pallas kernels for 0% -> 0%
where the time goes in v1:
time: 110 us
  Pallas kernels  107 us (97%)
  local copies, waits for them, and re-layouts  3.21 us (3%)
    pallas_call x1, Pallas kernels, gathered(): pl.pallas_call(gather_kernel, out_shape=jax.ShapeDtypeStruct((seqs, half,...  101 us
    pallas_call x1, Pallas kernels, shards(): pl.pallas_call(functools.partial(turn_kernel, scale=length ** (-0.5)), ou...  5.64 us
    unnamed x2, local copies, waits for them, and re-layouts  3.21 us

profile of v1, /device:TPU:1, one launch (start us, length us, event | category | flops | bytes accessed | tf_op | source)
XLA Modules:
  0.0 110.2 jit_solution(6370842320137689642)
XLA Ops:
  0.0 1.5 %copy.5 = f32[16,8,8]{2,1,0:T(8,128)} copy(f32[16,8,8]{0,2,1:T(8,128)} %param.6) | data formatting | bytes 8192 | tf_op args[2]
  1.5 1.8 %copy.6 = f32[128,8,8]{2,1,0:T(8,128)} copy(f32[128,8,8]{0,2,1:T(8,128)} %param.7) | data formatting | bytes 65536 | tf_op args[3]
  3.2 101.3 %gathered.1.corr = bf16[3,128,1024]{2,1,0:T(8,128)(2,1)} custom-call(bf16[3,64,8192]{2,1,0:T(8,128)(2,1)} %acts.1, bf16[3,64,1024]{2,1,0:T(8,128)(2,1)} %grads.1), custom_call_target="tpu_custom_call" | custom-call | tf_op jit(solution)/shard_map/gathered/pallas_call | solution.py:270
  104.5 5.6 %turned.1 = f32[1024,128]{1,0:T(8,128)} custom-call(bf16[3,128,1024]{2,1,0:T(8,128)(2,1)} %gathered.1.corr, f32[128,8]{1,0:T(8,128)} %bitcast.3, f32[1024,8]{1,0:T(8,128)} %bitcast.2), custom_call_target="tpu_custom_call" | custom-call | tf_op jit(solution)/shard_map/turned/pallas_call | solution.py:338

commit v2 on v0

v2 whole, which is shorter than its diff:
```python
import functools

import jax
import jax.numpy as jnp
from jax import lax
from jax.experimental import pallas as pl
from jax.experimental.pallas import tpu as pltpu
from jax.sharding import PartitionSpec as P

MESH = pl.DeviceIdType.MESH
Y, Z, X = 4, 8, 4
PIECE = 256
BF16, F32 = jnp.bfloat16, jnp.float32


def halves(v):
    high = v.astype(BF16)
    return high, (v - high.astype(F32)).astype(BF16)


def dot(a, b):
    return jnp.dot(a, b, preferred_element_type=F32)


def iota(shape, dim):
    return lax.broadcasted_iota(jnp.int32, shape, dim)


def spread(flat, j, size):
    blocks = flat.shape[1]
    first = j * (size // 8)
    repeat = (iota((size, blocks), 1) == first + lax.div(iota((size, blocks), 0), 8)).astype(BF16)
    mine = lax.div(iota((size, 64), 1), 8) == lax.rem(iota((size, 64), 0), 8)
    fold = (lax.rem(iota((64, size), 1), 8) == lax.rem(iota((64, size), 0), 8)).astype(BF16)
    diagonal = lax.div(iota((size, size), 0), 8) == lax.div(iota((size, size), 1), 8)
    parts = []
    for part in halves(flat):
        rows = lax.dot_general(repeat, part, (((1,), (1,)), ((), ())), preferred_element_type=F32)
        rows = jnp.where(mine, rows, 0.0).astype(BF16)
        parts.append(jnp.where(diagonal, dot(rows, fold), 0.0).astype(BF16))
    return parts


def kernel(
    acts, grads, act_basis, grad_basis, out,
    a2, a_all, a_t, g_all, snd, rly, rcv, nxt, own, fin, landed, acc, result, act_flat, grad_flat, act_diag, grad_diag,
    a_send, a_recv, w_send, r_send, g_recv, k_send, k_recv,
    x_send, x_recv, v_send, q_send, q_recv, y_send, y_recv, f_send, f_recv, b_sem, o_sem,
    *, scale,
):
    seqs, rows, _ = acts.shape
    units = grads.shape[2]
    pieces = units // PIECE
    stages = seqs * pieces
    width = a2.shape[-1]
    half = width // 2
    depth = 2 * Z * rows
    tok, place = lax.axis_index("tok"), lax.axis_index("out")
    xh, z, y = lax.rem(tok, 2), lax.rem(lax.div(tok, 2), Z), lax.div(tok, 2 * Z)
    c, xl = lax.rem(place, 2), lax.div(place, 2)
    x = 2 * xh + xl
    sgn = 1 - 2 * c
    chunk = 2 * xl + c

    def dev(xi, yi, zi, ci):
        return ((yi * Z + zi) * 2 + lax.div(xi, 2), 2 * lax.rem(xi, 2) + ci)

    swapped = ((y * Z + z) * 2 + c, 2 * xl + xh)
    stays = xh == c
    moves = jnp.logical_not(stays)

    def remote(src, dst, send, recv, device):
        return pltpu.make_async_remote_copy(
            src_ref=src, dst_ref=dst, send_sem=send, recv_sem=recv,
            device_id=device, device_id_type=MESH,
        )

    def local(src, dst, sem):
        return pltpu.make_async_copy(src, dst, sem)

    def arrived(ref, sem):
        local(ref, ref, sem).wait()

    local(act_basis, act_flat, b_sem.at[0]).start()
    local(grad_basis, grad_flat, b_sem.at[1]).start()
    barrier = pltpu.get_barrier_semaphore()

    def greet(device):
        pl.semaphore_signal(barrier, inc=1, device_id=device, device_id_type=MESH)

    @pl.loop(1, Z)
    def _(d):
        greet(dev(x, y, lax.rem(z + d, Z), c))

    @pl.loop(1, Y)
    def _(d):
        greet(dev(x, lax.rem(y + d, Y), z, c))

    @pl.loop(1, 2 * X)
    def _(d):
        greet(dev(lax.rem(x + lax.div(d, 2), X), y, z, lax.rem(c + d, 2)))

    pl.semaphore_wait(barrier, (Z - 1) + (Y - 1) + (2 * X - 1))

    def a2a_view(s, zt):
        return acts.at[s, :, pl.ds(pl.multiple_of((chunk * Z + zt) * width, width), width)]

    def a2a(s, d):
        for step in {d, Z - d}:
            zt = lax.rem(z + step, Z)
            remote(a2a_view(s, zt), a2.at[s, z], a_send.at[s], a_recv.at[s, z], dev(x, y, zt, c)).start()

    def grads_view(j):
        s, h = lax.div(j, pieces), lax.rem(j, pieces)
        return grads.at[s, :, pl.ds(pl.multiple_of(h * PIECE, PIECE), PIECE)]

    def block(k):
        return lax.rem(z + k * sgn + Z, Z)

    def ring(j, zz, direction, sem):
        return remote(g_all.at[j, c, zz], g_all.at[j, c, zz], sem, g_recv.at[j, zz],
                      dev(x, y, lax.rem(z + direction + Z, Z), c))

    def long(j, k):
        return ring(j, block(-k), sgn, r_send.at[j])

    def short(j, k):
        return ring(j, block(k), -sgn, r_send.at[j])

    def across(j):
        return remote(g_all.at[j, c], g_all.at[j, c], k_send.at[j], k_recv.at[j], dev(x, y, z, 1 - c))

    def hop(j, k):
        zz = block(-k)
        arrived(g_all.at[j, c, zz], g_recv.at[j, zz])
        if k < 4:
            long(j, k).start()
            if k > 0:
                zz = block(k)
                arrived(g_all.at[j, c, zz], g_recv.at[j, zz])
            if k < 3:
                short(j, k).start()
        else:
            across(j).start()

    def x_copy(s, d):
        h = lax.rem(c + d, 2)
        cols = pl.ds(pl.multiple_of(h * half, half), half)
        return remote(a2.at[s, :, :, cols], a_all.at[s, 2 * chunk + xh], x_send.at[s],
                      x_recv.at[s, 2 * chunk + xh], dev(lax.rem(x + lax.div(d, 2), X), y, z, h))

    direct = (2, 3, 6, 7, 1)

    def xsend(s):
        @pl.loop(0, Z)
        def _(zz):
            arrived(a2.at[s, zz], a_recv.at[s, zz])

        for d in direct:
            x_copy(s, d).start()

        cols = pl.ds(pl.multiple_of(c * half, half), half)
        local(a2.at[s, :, :, cols], a_all.at[s, 2 * chunk + xh], x_recv.at[s, 2 * chunk + xh]).start()

    def slot(dx, ci):
        xi = lax.rem(x + dx, X)
        return 2 * (2 * lax.rem(xi, 2) + ci) + lax.div(xi, 2)

    passing = ((X - 1, 0, 1), (1, 1, X - 1))

    def pass_copy(s, i):
        dx, ci, to = passing[i]
        u = slot(dx, ci)
        return remote(a_all.at[s, u], a_all.at[s, u], v_send.at[s, i], x_recv.at[s, u],
                      dev(lax.rem(x + to, X), y, z, c))

    def xpass(s):
        for i, (dx, ci, to) in enumerate(passing):
            u = slot(dx, ci)
            arrived(a_all.at[s, u], x_recv.at[s, u])
            pass_copy(s, i).start()

    def xrest(s):
        for dx in range(X):
            for ci in range(2):
                if (dx, ci) in ((X - 1, 0), (1, 1)):
                    continue
                u = slot(dx, ci)
                arrived(a_all.at[s, u], x_recv.at[s, u])
        for i, yi in enumerate((far, behind, ahead, y)):
            a_t[i * half:(i + 1) * half, :] = a_all[s, pl.ds(2 * yi, 2)].reshape(depth, half).T

    ahead, behind, far = lax.rem(y + sgn + Y, Y), lax.rem(y - sgn + Y, Y), lax.rem(y + 2, Y)

    def far_copy(j):
        return remote(snd.at[j, 0], rly.at[j], q_send.at[j], q_recv.at[j], dev(x, ahead, z, c))

    def behind_copy(j):
        return remote(snd.at[j, 1], rcv.at[j, 0], y_send.at[j, 0], y_recv.at[j, 0], dev(x, behind, z, c))

    def ahead_copy(j):
        return remote(snd.at[j, 2], rcv.at[j, 1], y_send.at[j, 1], y_recv.at[j, 1], dev(x, ahead, z, c))

    def multiply(j):
        @pl.when(lax.rem(j, pieces) == 0)
        def _():
            xrest(lax.div(j, pieces))

        arrived(g_all.at[j, 1 - c], k_recv.at[j])
        product = dot(a_t[...], g_all[j].reshape(depth, PIECE))
        snd[j, 0] = product[:half].astype(BF16)
        snd[j, 1] = product[half:2 * half].astype(BF16)
        nxt[j] = product[2 * half:3 * half]
        own[j] = product[3 * half:]
        far_copy(j).start()
        behind_copy(j).start()

    def relay(j):
        arrived(rly.at[j], q_recv.at[j])
        snd[j, 2] = (nxt[j] + rly[j].astype(F32)).astype(BF16)
        ahead_copy(j).start()

    def f_copy(j):
        return remote(fin.at[j], landed.at[j], f_send.at[j], f_recv.at[j], swapped)

    def reduce(j):
        for i in range(2):
            arrived(rcv.at[j, i], y_recv.at[j, i])
        total = own[j] + (rcv[j, 0].astype(F32) + rcv[j, 1].astype(F32))
        fin[j] = total.astype(BF16)

        @pl.when(stays)
        def _():
            local(fin.at[j], landed.at[j], f_recv.at[j]).start()

        @pl.when(moves)
        def _():
            f_copy(j).start()

    def out_copy(h):
        view = pl.ds(pl.multiple_of(h * PIECE, PIECE), PIECE)
        return local(result.at[view], out.at[view], o_sem.at[h])

    def finish(j):
        s, h = lax.div(j, pieces), lax.rem(j, pieces)
        arrived(landed.at[j], f_recv.at[j])
        piece = landed[j]
        high, low = halves(dot(jnp.concatenate([piece, piece], axis=1), grad_diag[h]))
        turned = dot(act_diag[...], jnp.concatenate([high, low, high], axis=0)) * scale
        square = turned * turned

        @pl.when(s == 0)
        def _():
            acc[h] = square

        @pl.when(s > 0)
        def _():
            acc[h] = acc[h] + square

        @pl.when(s == seqs - 1)
        def _():
            start = pl.multiple_of(h * PIECE, PIECE)
            for i in range(PIECE // 128):
                result[pl.ds(start + i * 128, 128), :] = acc[h, :, i * 128:(i + 1) * 128].T
            out_copy(h).start()

    def drain(j):
        arrived(g_all.at[j, c, pl.ds(0, Z - 1)], r_send.at[j])
        across(j).wait_send()
        far_copy(j).wait_send()
        behind_copy(j).wait_send()
        ahead_copy(j).wait_send()

        @pl.when(moves)
        def _():
            arrived(g_all.at[j, c, 0], w_send.at[j])
            f_copy(j).wait_send()

    def prepare():
        arrived(act_flat, b_sem.at[0])
        arrived(grad_flat, b_sem.at[1])
        high, low = spread(act_flat[...].reshape(64, half // 8), 0, half)
        high, low = high.T, low.T
        for i, part in enumerate((high, high, low)):
            act_diag[:, i * half:(i + 1) * half] = part

        @pl.loop(0, pieces)
        def _(i):
            grad_diag[i, :PIECE], grad_diag[i, PIECE:] = spread(grad_flat[...].reshape(64, units // 8), i, PIECE)

    @pl.loop(0, stages)
    def _(j):
        @pl.when(stays)
        def _():
            local(grads_view(j), g_all.at[j, c, z], g_recv.at[j, z]).start()

        @pl.when(moves)
        def _():
            remote(grads_view(j), g_all.at[j, xh, z], w_send.at[j], g_recv.at[j, z], swapped).start()

    for s in range(seqs):
        local(a2a_view(s, z), a2.at[s, z], a_recv.at[s, z]).start()
    for d in (4, 3, 2, 1):
        a2a(0, d)

    def when_stage(j, step):
        @pl.when(jnp.logical_and(j >= 0, j < stages))
        def _():
            step(j)

    events = {
        1: (prepare,), 2: (lambda: xsend(0), lambda: a2a(1, 4)), 3: (lambda: a2a(1, 3),), 4: (lambda: a2a(1, 2), lambda: xpass(0)), 5: (lambda: a2a(1, 1),),
        6: (lambda: a2a(2, 4),), 7: (lambda: a2a(2, 3),), 8: (lambda: xsend(1), lambda: a2a(2, 2)), 9: (lambda: a2a(2, 1),), 10: (lambda: xpass(1),),
        12: (lambda: xsend(2),), 14: (lambda: xpass(2),),
    }

    @pl.loop(0, stages + 20)
    def _(tick):
        for k in (4, 3, 2, 1, 0):
            when_stage(tick - 2 * k, functools.partial(hop, k=k))
        for t, calls in events.items():
            @pl.when(tick == t)
            def _():
                for call in calls:
                    call()
        when_stage(tick - 9, multiply)
        when_stage(tick - 11, relay)
        when_stage(tick - 13, reduce)
        when_stage(tick - 16, finish)
        when_stage(tick - 19, drain)

    @pl.loop(0, seqs)
    def _(s):
        arrived(a2.at[s, pl.ds(0, Z - 1)], a_send.at[s])
        arrived(a_all.at[s, pl.ds(0, len(direct))], x_send.at[s])
        for i in range(len(passing)):
            pass_copy(s, i).wait_send()

    @pl.loop(0, pieces)
    def _(h):
        out_copy(h).wait()


def shards(acts, grads, act_basis, grad_basis):
    seqs, rows, inputs = acts.shape
    units = grads.shape[2]
    width = inputs // (Y * Z)
    half = width // 2
    pieces = units // PIECE
    stages = seqs * pieces
    length = rows * Y * Z * 2
    dma = pltpu.SemaphoreType.DMA
    return pl.pallas_call(
        functools.partial(kernel, scale=length ** -0.5),
        out_shape=jax.ShapeDtypeStruct((units, half), F32),
        in_specs=[pl.BlockSpec(memory_space=pl.ANY)] * 4,
        out_specs=pl.BlockSpec(memory_space=pl.ANY),
        scratch_shapes=[
            pltpu.VMEM((seqs, Z, rows, width), BF16),
            pltpu.VMEM((seqs, 2 * Y, Z, rows, half), BF16),
            pltpu.VMEM((Y * half, 2 * Z * rows), BF16),
            pltpu.VMEM((stages, 2, Z, rows, PIECE), BF16),
            pltpu.VMEM((stages, 3, half, PIECE), BF16),
            pltpu.VMEM((stages, half, PIECE), BF16),
            pltpu.VMEM((stages, 2, half, PIECE), BF16),
            pltpu.VMEM((stages, half, PIECE), F32),
            pltpu.VMEM((stages, half, PIECE), F32),
            pltpu.VMEM((stages, half, PIECE), BF16),
            pltpu.VMEM((stages, half, PIECE), BF16),
            pltpu.VMEM((pieces, half, PIECE), F32),
            pltpu.VMEM((units, half), F32),
            pltpu.VMEM((8, 8, half // 8), F32),
            pltpu.VMEM((8, 8, units // 8), F32),
            pltpu.VMEM((half, 3 * half), BF16),
            pltpu.VMEM((pieces, 2 * PIECE, PIECE), BF16),
            dma((seqs,)), dma((seqs, Z)), dma((stages,)),
            dma((stages,)), dma((stages, Z)),
            dma((stages,)), dma((stages,)),
            dma((seqs,)), dma((seqs, 2 * Y)), dma((seqs, 2)),
            dma((stages,)), dma((stages,)), dma((stages, 2)), dma((stages, 2)),
            dma((stages,)), dma((stages,)), dma((2,)), dma((pieces,)),
        ],
        compiler_params=pltpu.CompilerParams(
            collective_id=0, has_side_effects=True, vmem_limit_bytes=56 << 20
        ),
        name="gathered",
    )(acts, grads, act_basis.transpose(1, 2, 0), grad_basis.transpose(1, 2, 0))


def solution(mesh):
    placed = (
        P(None, "tok", None),
        P(None, "tok", "out"),
        P("tok", None, None),
        P("out", None, None),
    )
    return jax.shard_map(
        shards, mesh=mesh, in_specs=placed, out_specs=P("out", "tok"), check_vma=False
    )
```

time: 360 us -> 88.7 us (0.25)
  waiting for transfers between devices: 244 us -> 0 us
  Pallas kernels: 0 us -> 86.6 us
  local copies, waits for them, and re-layouts: 65.4 us -> 1.87 us
  matrix products: 19.2 us -> 0 us
  starting transfers between devices: 15.4 us -> 0 us
  between operations: 13.5 us -> 0.01 us
    all_gather x1 -> x0, waiting for transfers between devices: 150 us -> none  [shards(): lax.all_gather(turned_grads, 'tok', axis=1, tiled=True)]
    all_to_all x1 -> x0, waiting for transfers between devices: 94.4 us -> none  [shards(): lax.all_to_all(acts, 'tok', split_axis=2, concat_axis=1, tiled=True)]
    pallas_call x0 -> x1, Pallas kernels: none -> 86.6 us  [shards(): pl.pallas_call(functools.partial(kernel, scale=length ** (-0.5)), out_sha...]
    unnamed x7 -> x1, local copies, waits for them, and re-layouts: 35 us -> 1.87 us
    dot_general x5 -> x0, matrix products: 19.2 us -> none  [the longest x1 14.5 us: shards(): jnp.einsum('sto,sti->soi', lax.all_gather(turned_grads, 'tok', axis=1, ti...]
    all_to_all x1 -> x0, starting transfers between devices: 15.4 us -> none  [shards(): lax.all_to_all(acts, 'tok', split_axis=2, concat_axis=1, tiled=True)]
    mul x5 -> x0, local copies, waits for them, and re-layouts: 11.9 us -> none  [rotate_local(): blocks[:, :, :, None, :] * identity[None, :, None, :, None]]
    all_to_all x1 -> x0, local copies, waits for them, and re-layouts: 10.5 us -> none  [shards(): lax.all_to_all(acts, 'tok', split_axis=2, concat_axis=1, tiled=True)]
  transfers between devices with their start and end apart: 2 -> 0, of which waited for: 2 -> 0; matrix products, arithmetic and copies ran while one was open for 16% -> 0% of each run, Pallas kernels for 0% -> 0%
where the time goes in v2:
time: 88.7 us; the launch traced here: 88.5 us
  Pallas kernels  86.6 us (98%)
  local copies, waits for them, and re-layouts  1.87 us (2%)
    pallas_call x1, Pallas kernels, shards(): pl.pallas_call(functools.partial(kernel, scale=length ** (-0.5)), out_sha...  86.6 us
    unnamed x1, local copies, waits for them, and re-layouts  1.87 us

profile of v2, /device:TPU:1, one launch (start us, length us, event | category | flops | bytes accessed | tf_op | source)
XLA Modules:
  0.0 88.5 jit_solution(11264638067824702574)
XLA Ops:
  0.0 86.6 %gathered.1 = f32[1024,128]{1,0:T(8,128)} custom-call(bf16[3,64,8192]{2,1,0:T(8,128)(2,1)} %acts.1, bf16[3,64,1024]{2,1,0:T(8,128)(2,1)} %grads.1, f32[8,8,16]{2,1,0:T(8,128)} %bitcast.2, f32[8,8,128]{2,1,0:T(8,128)} %bitcast.3), custom_call_target="tpu_custom_call" | custom-call | tf_op jit(solution)/shard_map/gathered/pallas_call | solution.py:353
  86.6 1.9 %copy.6 = f32[1024,128]{1,0:T(8,128)} copy(f32[1024,128]{1,0:T(8,128)} %gathered.1) | data formatting | bytes 1048576

commit v3 on v2

--- a/solution.py
+++ b/solution.py
@@ -20,6 +20,14 @@
 
 def dot(a, b):
     return jnp.dot(a, b, preferred_element_type=F32)
+
+
+def over(a, n):
+    return jnp.right_shift(a, n.bit_length() - 1)
+
+
+def mod(a, n):
+    return jnp.bitwise_and(a, n - 1)
 
 
 def iota(shape, dim):
@@ -56,14 +64,14 @@
     half = width // 2
     depth = 2 * Z * rows
     tok, place = lax.axis_index("tok"), lax.axis_index("out")
-    xh, z, y = lax.rem(tok, 2), lax.rem(lax.div(tok, 2), Z), lax.div(tok, 2 * Z)
-    c, xl = lax.rem(place, 2), lax.div(place, 2)
+    xh, z, y = mod(tok, 2), mod(over(tok, 2), Z), over(tok, 2 * Z)
+    c, xl = mod(place, 2), over(place, 2)
     x = 2 * xh + xl
     sgn = 1 - 2 * c
     chunk = 2 * xl + c
 
     def dev(xi, yi, zi, ci):
-        return ((yi * Z + zi) * 2 + lax.div(xi, 2), 2 * lax.rem(xi, 2) + ci)
+        return ((yi * Z + zi) * 2 + over(xi, 2), 2 * mod(xi, 2) + ci)
 
     swapped = ((y * Z + z) * 2 + c, 2 * xl + xh)
     stays = xh == c
@@ -90,15 +98,15 @@
 
     @pl.loop(1, Z)
     def _(d):
-        greet(dev(x, y, lax.rem(z + d, Z), c))
+        greet(dev(x, y, mod(z + d, Z), c))
 
     @pl.loop(1, Y)
     def _(d):
-        greet(dev(x, lax.rem(y + d, Y), z, c))
+        greet(dev(x, mod(y + d, Y), z, c))
 
     @pl.loop(1, 2 * X)
     def _(d):
-        greet(dev(lax.rem(x + lax.div(d, 2), X), y, z, lax.rem(c + d, 2)))
+        greet(dev(mod(x + over(d, 2), X), y, z, mod(c + d, 2)))
 
     pl.semaphore_wait(barrier, (Z - 1) + (Y - 1) + (2 * X - 1))
 
@@ -107,64 +115,68 @@
 
     def a2a(s, d):
         for step in {d, Z - d}:
-            zt = lax.rem(z + step, Z)
+            zt = mod(z + step, Z)
             remote(a2a_view(s, zt), a2.at[s, z], a_send.at[s], a_recv.at[s, z], dev(x, y, zt, c)).start()
 
     def grads_view(j):
-        s, h = lax.div(j, pieces), lax.rem(j, pieces)
+        s, h = over(j, pieces), mod(j, pieces)
         return grads.at[s, :, pl.ds(pl.multiple_of(h * PIECE, PIECE), PIECE)]
 
     def block(k):
-        return lax.rem(z + k * sgn + Z, Z)
-
-    def ring(j, zz, direction, sem):
-        return remote(g_all.at[j, c, zz], g_all.at[j, c, zz], sem, g_recv.at[j, zz],
-                      dev(x, y, lax.rem(z + direction + Z, Z), c))
+        return mod(z + k * sgn, Z)
+
+    forth, back, partner = dev(x, y, mod(z + sgn, Z), c), dev(x, y, mod(z - sgn, Z), c), dev(x, y, z, 1 - c)
+
+    def ring(j, zz, to, sem):
+        return remote(g_all.at[j, c, zz], g_all.at[j, c, zz], sem, g_recv.at[j, zz], to)
 
     def long(j, k):
-        return ring(j, block(-k), sgn, r_send.at[j])
+        return ring(j, block(-k), forth, r_send.at[j])
 
     def short(j, k):
-        return ring(j, block(k), -sgn, r_send.at[j])
+        return ring(j, block(k), back, r_send.at[j])
 
     def across(j):
-        return remote(g_all.at[j, c], g_all.at[j, c], k_send.at[j], k_recv.at[j], dev(x, y, z, 1 - c))
+        return remote(g_all.at[j, c], g_all.at[j, c], k_send.at[j], k_recv.at[j], partner)
 
     def hop(j, k):
         zz = block(-k)
         arrived(g_all.at[j, c, zz], g_recv.at[j, zz])
-        if k < 4:
-            long(j, k).start()
-            if k > 0:
-                zz = block(k)
-                arrived(g_all.at[j, c, zz], g_recv.at[j, zz])
-            if k < 3:
-                short(j, k).start()
-        else:
-            across(j).start()
+        long(j, k).start()
+        if k > 0:
+            zz = block(k)
+            arrived(g_all.at[j, c, zz], g_recv.at[j, zz])
+        if k < 3:
+            short(j, k).start()
+
+    def last_hop(j):
+        zz = block(-4)
+        arrived(g_all.at[j, c, zz], g_recv.at[j, zz])
+        across(j).start()
 
     def x_copy(s, d):
-        h = lax.rem(c + d, 2)
+        h = mod(c + d, 2)
         cols = pl.ds(pl.multiple_of(h * half, half), half)
         return remote(a2.at[s, :, :, cols], a_all.at[s, 2 * chunk + xh], x_send.at[s],
-                      x_recv.at[s, 2 * chunk + xh], dev(lax.rem(x + lax.div(d, 2), X), y, z, h))
-
-    direct = (2, 3, 6, 7, 1)
+                      x_recv.at[s, 2 * chunk + xh], dev(mod(x + over(d, 2), X), y, z, h))
+
+    direct = 5
 
     def xsend(s):
         @pl.loop(0, Z)
         def _(zz):
             arrived(a2.at[s, zz], a_recv.at[s, zz])
 
-        for d in direct:
-            x_copy(s, d).start()
+        for d in (2, 3, 6, 7):
+            x_copy(s, mod(d + 4 * c, 2 * X)).start()
+        x_copy(s, 1).start()
 
         cols = pl.ds(pl.multiple_of(c * half, half), half)
         local(a2.at[s, :, :, cols], a_all.at[s, 2 * chunk + xh], x_recv.at[s, 2 * chunk + xh]).start()
 
     def slot(dx, ci):
-        xi = lax.rem(x + dx, X)
-        return 2 * (2 * lax.rem(xi, 2) + ci) + lax.div(xi, 2)
+        xi = mod(x + dx, X)
+        return 2 * (2 * mod(xi, 2) + ci) + over(xi, 2)
 
     passing = ((X - 1, 0, 1), (1, 1, X - 1))
 
@@ -172,7 +184,7 @@
         dx, ci, to = passing[i]
         u = slot(dx, ci)
         return remote(a_all.at[s, u], a_all.at[s, u], v_send.at[s, i], x_recv.at[s, u],
-                      dev(lax.rem(x + to, X), y, z, c))
+                      dev(mod(x + to, X), y, z, c))
 
     def xpass(s):
         for i, (dx, ci, to) in enumerate(passing):
@@ -188,26 +200,26 @@
                 u = slot(dx, ci)
                 arrived(a_all.at[s, u], x_recv.at[s, u])
         for i, yi in enumerate((far, behind, ahead, y)):
-            a_t[i * half:(i + 1) * half, :] = a_all[s, pl.ds(2 * yi, 2)].reshape(depth, half).T
-
-    ahead, behind, far = lax.rem(y + sgn + Y, Y), lax.rem(y - sgn + Y, Y), lax.rem(y + 2, Y)
+            a_t[s % 2, i * half:(i + 1) * half, :] = a_all[s, pl.ds(2 * yi, 2)].reshape(depth, half).T
+
+    ahead, behind, far = mod(y + sgn, Y), mod(y - sgn, Y), mod(y + 2, Y)
+    up, down = dev(x, ahead, z, c), dev(x, behind, z, c)
 
     def far_copy(j):
-        return remote(snd.at[j, 0], rly.at[j], q_send.at[j], q_recv.at[j], dev(x, ahead, z, c))
+        return remote(snd.at[j, 0], rly.at[j], q_send.at[j], q_recv.at[j], up)
 
     def behind_copy(j):
-        return remote(snd.at[j, 1], rcv.at[j, 0], y_send.at[j, 0], y_recv.at[j, 0], dev(x, behind, z, c))
+        return remote(snd.at[j, 1], rcv.at[j, 0], y_send.at[j, 0], y_recv.at[j, 0], down)
 
     def ahead_copy(j):
-        return remote(snd.at[j, 2], rcv.at[j, 1], y_send.at[j, 1], y_recv.at[j, 1], dev(x, ahead, z, c))
+        return remote(snd.at[j, 2], rcv.at[j, 1], y_send.at[j, 1], y_recv.at[j, 1], up)
 
     def multiply(j):
-        @pl.when(lax.rem(j, pieces) == 0)
-        def _():
-            xrest(lax.div(j, pieces))
+        if j % pieces == 0:
+            xrest(j // pieces)
 
         arrived(g_all.at[j, 1 - c], k_recv.at[j])
-        product = dot(a_t[...], g_all[j].reshape(depth, PIECE))
+        product = dot(a_t[j // pieces % 2], g_all[j].reshape(depth, PIECE))
         snd[j, 0] = product[:half].astype(BF16)
         snd[j, 1] = product[half:2 * half].astype(BF16)
         nxt[j] = product[2 * half:3 * half]
@@ -238,30 +250,22 @@
             f_copy(j).start()
 
     def out_copy(h):
-        view = pl.ds(pl.multiple_of(h * PIECE, PIECE), PIECE)
+        view = pl.ds(h * PIECE, PIECE)
         return local(result.at[view], out.at[view], o_sem.at[h])
 
     def finish(j):
-        s, h = lax.div(j, pieces), lax.rem(j, pieces)
+        s, h = divmod(j, pieces)
         arrived(landed.at[j], f_recv.at[j])
         piece = landed[j]
         high, low = halves(dot(jnp.concatenate([piece, piece], axis=1), grad_diag[h]))
         turned = dot(act_diag[...], jnp.concatenate([high, low, high], axis=0)) * scale
         square = turned * turned
-
-        @pl.when(s == 0)
-        def _():
+        if s > 0:
+            square = acc[h] + square
+        if s < seqs - 1:
             acc[h] = square
-
-        @pl.when(s > 0)
-        def _():
-            acc[h] = acc[h] + square
-
-        @pl.when(s == seqs - 1)
-        def _():
-            start = pl.multiple_of(h * PIECE, PIECE)
-            for i in range(PIECE // 128):
-                result[pl.ds(start + i * 128, 128), :] = acc[h, :, i * 128:(i + 1) * 128].T
+        else:
+            result[h * PIECE:(h + 1) * PIECE, :] = square.T
             out_copy(h).start()
 
     def drain(j):
@@ -303,41 +307,39 @@
     for d in (4, 3, 2, 1):
         a2a(0, d)
 
-    def when_stage(j, step):
-        @pl.when(jnp.logical_and(j >= 0, j < stages))
-        def _():
-            step(j)
-
-    events = {
-        1: (prepare,), 2: (lambda: xsend(0), lambda: a2a(1, 4)), 3: (lambda: a2a(1, 3),), 4: (lambda: a2a(1, 2), lambda: xpass(0)), 5: (lambda: a2a(1, 1),),
-        6: (lambda: a2a(2, 4),), 7: (lambda: a2a(2, 3),), 8: (lambda: xsend(1), lambda: a2a(2, 2)), 9: (lambda: a2a(2, 1),), 10: (lambda: xpass(1),),
-        12: (lambda: xsend(2),), 14: (lambda: xpass(2),),
-    }
-
-    @pl.loop(0, stages + 20)
-    def _(tick):
-        for k in (4, 3, 2, 1, 0):
-            when_stage(tick - 2 * k, functools.partial(hop, k=k))
-        for t, calls in events.items():
-            @pl.when(tick == t)
-            def _():
-                for call in calls:
-                    call()
-        when_stage(tick - 9, multiply)
-        when_stage(tick - 11, relay)
-        when_stage(tick - 13, reduce)
-        when_stage(tick - 16, finish)
-        when_stage(tick - 19, drain)
+    plan = []
+
+    def put(at, step, *args):
+        plan.append((at, len(plan), step, args))
+
+    put(0.9, prepare)
+    for s, sends, go, through in ((0, (), 0.99, 3.1), (1, (3.3, 3.8, 4.3, 4.7), 6.45, 8.1), (2, (5.1, 5.6, 6.1, 6.5), 8.5, 11.1)):
+        for at, d in zip(sends, (4, 3, 2, 1)):
+            put(at, a2a, s, d)
+        put(go, xsend, s)
+        put(through, xpass, s)
+    for j in range(stages):
+        first = j < pieces
+        for k in range(4):
+            put(k + j / pieces if first else j - pieces + 1 + 2 * k + (4 - k) / 10, hop, j, k)
+        put(4 + j / 10 if first else j + 5, last_hop, j)
+        put(4.6 + 0.3 * j if first else j + 5.9, multiply, j)
+        put(6.2 + 0.3 * j if first else j + 7.92, relay, j)
+        put(8.7 + 0.5 * j if first else j + 10.1, reduce, j)
+        put(max(j + 13.2, 17.2 + j / 2), finish, j)
+        put(j + 14.5, drain, j)
+
+    for _, _, step, args in sorted(plan, key=lambda call: call[:2]):
+        step(*args)
 
     @pl.loop(0, seqs)
     def _(s):
         arrived(a2.at[s, pl.ds(0, Z - 1)], a_send.at[s])
-        arrived(a_all.at[s, pl.ds(0, len(direct))], x_send.at[s])
+        arrived(a_all.at[s, pl.ds(0, direct)], x_send.at[s])
         for i in range(len(passing)):
             pass_copy(s, i).wait_send()
 
-    @pl.loop(0, pieces)
-    def _(h):
+    for h in range(pieces):
         out_copy(h).wait()
 
 
@@ -358,7 +360,7 @@
         scratch_shapes=[
             pltpu.VMEM((seqs, Z, rows, width), BF16),
             pltpu.VMEM((seqs, 2 * Y, Z, rows, half), BF16),
-            pltpu.VMEM((Y * half, 2 * Z * rows), BF16),
+            pltpu.VMEM((2, Y * half, 2 * Z * rows), BF16),
             pltpu.VMEM((stages, 2, Z, rows, PIECE), BF16),
             pltpu.VMEM((stages, 3, half, PIECE), BF16),
             pltpu.VMEM((stages, half, PIECE), BF16),

time: 88.7 us -> 86.6 us (0.976)
  Pallas kernels: 86.6 us -> 84.5 us
    pallas_call x1, Pallas kernels: 86.6 us -> 84.5 us  [shards(): pl.pallas_call(functools.partial(kernel, scale=length ** (-0.5)), out_sha...]
where the time goes in v3:
time: 86.6 us; the launch traced here: 86.4 us
  Pallas kernels  84.5 us (98%)
  local copies, waits for them, and re-layouts  1.87 us (2%)
    pallas_call x1, Pallas kernels, shards(): pl.pallas_call(functools.partial(kernel, scale=length ** (-0.5)), out_sha...  84.5 us
    unnamed x1, local copies, waits for them, and re-layouts  1.87 us

profile of v3, /device:TPU:1, one launch (start us, length us, event | category | flops | bytes accessed | tf_op | source)
XLA Modules:
  0.0 86.4 jit_solution(923281415860906762)
XLA Ops:
  0.0 84.5 %gathered.1 = f32[1024,128]{1,0:T(8,128)} custom-call(bf16[3,64,8192]{2,1,0:T(8,128)(2,1)} %acts.1, bf16[3,64,1024]{2,1,0:T(8,128)(2,1)} %grads.1, f32[8,8,16]{2,1,0:T(8,128)} %bitcast.2, f32[8,8,128]{2,1,0:T(8,128)} %bitcast.3), custom_call_target="tpu_custom_call" | custom-call | tf_op jit(solution)/shard_map/gathered/pallas_call | solution.py:355
  84.5 1.9 %copy.6 = f32[1024,128]{1,0:T(8,128)} copy(f32[1024,128]{1,0:T(8,128)} %gathered.1) | data formatting | bytes 1048576

commit v4 on v3

--- a/solution.py
+++ b/solution.py
@@ -313,7 +313,7 @@
         plan.append((at, len(plan), step, args))
 
     put(0.9, prepare)
-    for s, sends, go, through in ((0, (), 0.99, 3.1), (1, (3.3, 3.8, 4.3, 4.7), 6.45, 8.1), (2, (5.1, 5.6, 6.1, 6.5), 8.5, 11.1)):
+    for s, sends, go, through in ((0, (), 0.99, 3.1), (1, (2.9, 3.4, 3.9, 4.35), 5.7, 8.45), (2, (5.1, 5.6, 6.0, 6.35), 8.15, 11.3)):
         for at, d in zip(sends, (4, 3, 2, 1)):
             put(at, a2a, s, d)
         put(go, xsend, s)
@@ -324,7 +324,7 @@
             put(k + j / pieces if first else j - pieces + 1 + 2 * k + (4 - k) / 10, hop, j, k)
         put(4 + j / 10 if first else j + 5, last_hop, j)
         put(4.6 + 0.3 * j if first else j + 5.9, multiply, j)
-        put(6.2 + 0.3 * j if first else j + 7.92, relay, j)
+        put(6.95 + 0.35 * j if first else j + 7.92, relay, j)
         put(8.7 + 0.5 * j if first else j + 10.1, reduce, j)
         put(max(j + 13.2, 17.2 + j / 2), finish, j)
         put(j + 14.5, drain, j)

time: 86.6 us -> 91.4 us (1.055)
  Pallas kernels: 84.5 us -> 89.4 us
    pallas_call x1, Pallas kernels: 84.5 us -> 89.4 us  [shards(): pl.pallas_call(functools.partial(kernel, scale=length ** (-0.5)), out_sha...]
where the time goes in v4:
time: 91.4 us; the launch traced here: 91.2 us
  Pallas kernels  89.4 us (98%)
  local copies, waits for them, and re-layouts  1.87 us (2%)
    pallas_call x1, Pallas kernels, shards(): pl.pallas_call(functools.partial(kernel, scale=length ** (-0.5)), out_sha...  89.4 us
    unnamed x1, local copies, waits for them, and re-layouts  1.87 us

profile of v4, /device:TPU:1, one launch (start us, length us, event | category | flops | bytes accessed | tf_op | source)
XLA Modules:
  0.0 91.2 jit_solution(8051838557795007641)
XLA Ops:
  0.0 89.4 %gathered.1 = f32[1024,128]{1,0:T(8,128)} custom-call(bf16[3,64,8192]{2,1,0:T(8,128)(2,1)} %acts.1, bf16[3,64,1024]{2,1,0:T(8,128)(2,1)} %grads.1, f32[8,8,16]{2,1,0:T(8,128)} %bitcast.2, f32[8,8,128]{2,1,0:T(8,128)} %bitcast.3), custom_call_target="tpu_custom_call" | custom-call | tf_op jit(solution)/shard_map/gathered/pallas_call | solution.py:355
  89.4 1.9 %copy.6 = f32[1024,128]{1,0:T(8,128)} copy(f32[1024,128]{1,0:T(8,128)} %gathered.1) | data formatting | bytes 1048576

commit v5 on v3

--- a/solution.py
+++ b/solution.py
@@ -313,7 +313,7 @@
         plan.append((at, len(plan), step, args))
 
     put(0.9, prepare)
-    for s, sends, go, through in ((0, (), 0.99, 3.1), (1, (3.3, 3.8, 4.3, 4.7), 6.45, 8.1), (2, (5.1, 5.6, 6.1, 6.5), 8.5, 11.1)):
+    for s, sends, go, through in ((0, (), 0.99, 3.1), (1, (3.3, 3.8, 4.3, 4.7), 6.45, 8.45), (2, (5.1, 5.6, 6.1, 6.5), 8.35, 11.3)):
         for at, d in zip(sends, (4, 3, 2, 1)):
             put(at, a2a, s, d)
         put(go, xsend, s)

time: 86.6 us -> 92.4 us (1.067)
  Pallas kernels: 84.5 us -> 90.3 us
    pallas_call x1, Pallas kernels: 84.5 us -> 90.3 us  [shards(): pl.pallas_call(functools.partial(kernel, scale=length ** (-0.5)), out_sha...]
where the time goes in v5:
time: 92.4 us; the launch traced here: 92.2 us
  Pallas kernels  90.3 us (98%)
  local copies, waits for them, and re-layouts  1.87 us (2%)
    pallas_call x1, Pallas kernels, shards(): pl.pallas_call(functools.partial(kernel, scale=length ** (-0.5)), out_sha...  90.3 us
    unnamed x1, local copies, waits for them, and re-layouts  1.87 us

profile of v5, /device:TPU:1, one launch (start us, length us, event | category | flops | bytes accessed | tf_op | source)
XLA Modules:
  0.0 92.2 jit_solution(10082178404845046992)
XLA Ops:
  0.0 90.3 %gathered.1 = f32[1024,128]{1,0:T(8,128)} custom-call(bf16[3,64,8192]{2,1,0:T(8,128)(2,1)} %acts.1, bf16[3,64,1024]{2,1,0:T(8,128)(2,1)} %grads.1, f32[8,8,16]{2,1,0:T(8,128)} %bitcast.2, f32[8,8,128]{2,1,0:T(8,128)} %bitcast.3), custom_call_target="tpu_custom_call" | custom-call | tf_op jit(solution)/shard_map/gathered/pallas_call | solution.py:355
  90.3 1.9 %copy.6 = f32[1024,128]{1,0:T(8,128)} copy(f32[1024,128]{1,0:T(8,128)} %gathered.1) | data formatting | bytes 1048576

commit v6 on v4

--- a/solution.py
+++ b/solution.py
@@ -313,7 +313,7 @@
         plan.append((at, len(plan), step, args))
 
     put(0.9, prepare)
-    for s, sends, go, through in ((0, (), 0.99, 3.1), (1, (2.9, 3.4, 3.9, 4.35), 5.7, 8.45), (2, (5.1, 5.6, 6.0, 6.35), 8.15, 11.3)):
+    for s, sends, go, through in ((0, (), 0.99, 3.1), (1, (3.0, 3.5, 4.0, 4.4), 5.95, 7.95), (2, (5.1, 5.6, 6.0, 6.4), 8.45, 11.1)):
         for at, d in zip(sends, (4, 3, 2, 1)):
             put(at, a2a, s, d)
         put(go, xsend, s)

time: 91.4 us -> 87.2 us (0.954)
  Pallas kernels: 89.4 us -> 85.2 us
    pallas_call x1, Pallas kernels: 89.4 us -> 85.2 us  [shards(): pl.pallas_call(functools.partial(kernel, scale=length ** (-0.5)), out_sha...]
where the time goes in v6:
time: 87.2 us; the launch traced here: 87 us
  Pallas kernels  85.2 us (98%)
  local copies, waits for them, and re-layouts  1.87 us (2%)
    pallas_call x1, Pallas kernels, shards(): pl.pallas_call(functools.partial(kernel, scale=length ** (-0.5)), out_sha...  85.2 us
    unnamed x1, local copies, waits for them, and re-layouts  1.87 us

profile of v6, /device:TPU:1, one launch (start us, length us, event | category | flops | bytes accessed | tf_op | source)
XLA Modules:
  0.0 87.0 jit_solution(5913359913044599816)
XLA Ops:
  0.0 85.2 %gathered.1 = f32[1024,128]{1,0:T(8,128)} custom-call(bf16[3,64,8192]{2,1,0:T(8,128)(2,1)} %acts.1, bf16[3,64,1024]{2,1,0:T(8,128)(2,1)} %grads.1, f32[8,8,16]{2,1,0:T(8,128)} %bitcast.2, f32[8,8,128]{2,1,0:T(8,128)} %bitcast.3), custom_call_target="tpu_custom_call" | custom-call | tf_op jit(solution)/shard_map/gathered/pallas_call | solution.py:355
  85.2 1.9 %copy.6 = f32[1024,128]{1,0:T(8,128)} copy(f32[1024,128]{1,0:T(8,128)} %gathered.1) | data formatting | bytes 1048576
